TPU v7x, 512 devices: a whole 4x4x16 slice. The times are simulated.
512 devices in a mesh: ctx: 32 (over x, z_lo, core), tp: 16 (over y, z_hi).
Axes of the slice: x: 4, y: 4, z: 16 (z_hi: 4, z_lo: 4; z = z_hi * 4 + z_lo), core: 2. Of those that a mesh axis runs over, the one named last changes fastest.
Arguments:
- queries: bfloat16 [8192, 4096], P('ctx', 'tp'), may hold values from -6 to 6
- keys: bfloat16 [8192, 512], P('ctx'), may hold values from -6 to 6
- values: bfloat16 [8192, 512], P('ctx'), may hold values from -6 to 6
- out_weight: bfloat16 [4096, 8192], P('tp'), may hold values from -0.125 to 0.125
- storm_mask: int32 [64, 64], replicated, may hold values from 0 to 1, as said below
Outputs:
- mixed: bfloat16 [8192, 8192], P('ctx', 'tp')
Inputs may be any that keep to these rules, and one draw needn't show every extreme that they name: storm_mask[i, j] is 0 where j > i and 1 where 0 <= i - j < 4.
All inputs are finite; a program needn't handle non-finite values.
Results may differ from a plain program's by a relative error of at most 0.019.
Values may be sent and summed in bfloat16 or wider, within the bound.
A program may use at most 64 MiB of HBM per device.

v0:
```python
import jax
import jax.numpy as jnp
from jax import lax
from jax.sharding import PartitionSpec as P

HDIM = 128
BLOCK = 128
GQ = 8


def rows_of_mask(index_of_block, storm_mask):
    blocks = storm_mask.shape[0]
    one_hot = (index_of_block[:, None] == jnp.arange(blocks)[None, :]).astype(jnp.float32)
    return jnp.dot(one_hot, storm_mask.astype(jnp.float32))


def update(carry, query, keys_part, values_part, first, row_mask):
    count = keys_part.shape[0]
    blocks = row_mask.shape[1]
    block_of = (first + jnp.arange(count)) // BLOCK
    one_hot = (jnp.arange(blocks)[:, None] == block_of[None, :]).astype(jnp.float32)
    allowed = jnp.dot(row_mask, one_hot) > 0.5

    def compute(state):
        maximum, total, running_total = state
        scores = jnp.einsum(
            "qhd,kd->hqk", query, keys_part, preferred_element_type=jnp.float32
        ) * HDIM ** (-0.5)
        scores = jnp.where(allowed[None], scores, -1e30)
        peak = jnp.maximum(maximum, jnp.max(scores, axis=2))
        weights = jnp.where(allowed[None], jnp.exp(scores - peak[:, :, None]), 0.0)
        factor = jnp.exp(maximum - peak)
        total = total * factor + jnp.sum(weights, axis=2)
        running_total = running_total * factor[:, :, None] + jnp.einsum(
            "hqk,kd->hqd",
            weights.astype(jnp.bfloat16),
            values_part,
            preferred_element_type=jnp.float32,
        )
        return (peak, total, running_total)

    return lax.cond(jnp.any(allowed), compute, lambda state: state, carry)


def body(queries, keys, values, out_weight, storm_mask):
    rows, width = queries.shape
    heads = width // HDIM
    place = lax.axis_index("ctx")
    shared_head = lax.axis_index("tp") * heads // GQ
    local_keys = lax.dynamic_slice_in_dim(keys, shared_head * HDIM, HDIM, 1)
    own_values = lax.dynamic_slice_in_dim(values, shared_head * HDIM, HDIM, 1)
    per_device = rows // BLOCK
    owned = place * per_device + jnp.arange(per_device)
    row_mask = jnp.repeat(rows_of_mask(owned, storm_mask), BLOCK, axis=0)
    query = queries.reshape(rows, heads, HDIM)
    initial = (
        jnp.full((heads, rows), -1e30, jnp.float32),
        jnp.zeros((heads, rows), jnp.float32),
        jnp.zeros((heads, rows, HDIM), jnp.float32),
    )
    carry = initial
    keys_part = lax.all_gather(local_keys, "ctx", axis=0, tiled=True)
    values_part = lax.all_gather(own_values, "ctx", axis=0, tiled=True)
    count = keys_part.shape[0]
    stride = 512

    def inner(state, number):
        first = number * stride
        keys_block = lax.dynamic_slice_in_dim(keys_part, first, stride, 0)
        values_block = lax.dynamic_slice_in_dim(values_part, first, stride, 0)
        return (update(state, query, keys_block, values_block, first, row_mask), None)

    carry, unused = lax.scan(inner, carry, jnp.arange(count // stride))
    maximum, total, running_total = carry
    attended = (
        (running_total / total[:, :, None])
        .astype(jnp.bfloat16)
        .transpose(1, 0, 2)
        .reshape(rows, width)
    )
    columns = out_weight.shape[1] // lax.axis_size("tp")
    whole = lax.psum(
        jnp.dot(attended, out_weight, preferred_element_type=jnp.float32).astype(jnp.bfloat16), "tp"
    ).astype(jnp.float32)
    result = lax.dynamic_slice_in_dim(whole, lax.axis_index("tp") * columns, columns, 1).astype(
        jnp.bfloat16
    )
    return result


def solution(mesh):
    placed = (P("ctx", "tp"), P("ctx", None), P("ctx", None), P("tp", None), P())
    return jax.shard_map(
        body, mesh=mesh, in_specs=placed, out_specs=P("ctx", "tp"), check_vma=False
    )
```

profile of v0, /device:TPU:4, one launch (start us, length us, event | category | flops | bytes accessed | tf_op | source)
XLA Modules:
  0.0 654.9 jit_solution(2344125904926054323)
XLA Ops:
  8.2 1.5 constant_dynamic-slice_fusion
  11.8 66.0 %all-gather.3.cloned.1.call-done = bf16[8192,128]{1,0:T(8,128)(2,1)} async-done(((bf16[256,128]{1,0:T(8,128)(2,1)}), bf16[8192,128]{1,0:T(8,128)(2,1)}) %all-gather.3.cloned.1.call-update) | async-done | bytes 2097168 | tf_op jit(solution)/shard_map/all_gather | solution.py:62
  77.8 66.0 %all-gather.5.cloned.1.call-done = bf16[8192,128]{1,0:T(8,128)(2,1)} async-done(((bf16[256,128]{1,0:T(8,128)(2,1)}), bf16[8192,128]{1,0:T(8,128)(2,1)}) %all-gather.5.cloned.1.call-update) | async-done | bytes 2097168 | tf_op jit(solution)/shard_map/all_gather | solution.py:63
  143.8 73.1 %while.17 = (s32[]{:T(128)}, f32[2,256]{1,0:T(2,128)S(1)}, f32[2,256]{1,0:T(2,128)S(1)}, f32[2,256,128]{2,1,0:T(8,128)S(1)}, s32[16]{0:T(128)S(1)}, /*index=5*/b...) while((s32[]{:T(128)}, f32[2,256]{1,0:T(2,128)S(1)}, ...), condition=%wide.region_6.7_spmd.clone, body=%wide.region_0.6_spmd.clone.sunk | while | flops 153822208 | bytes 4690489 | solution.py:73
  146.7 3.0 conditional.3
  148.2 1.4 convolution_add_fusion
  152.6 3.0 conditional.3
  154.1 1.4 convolution_add_fusion
  158.4 3.0 conditional.3
  160.0 1.4 convolution_add_fusion
  164.3 3.0 conditional.3
  165.8 1.4 convolution_add_fusion
  170.2 3.0 conditional.3
  171.7 1.4 convolution_add_fusion
  176.0 3.0 conditional.3
  177.6 1.4 convolution_add_fusion
  181.9 3.0 conditional.3
  183.4 1.4 convolution_add_fusion
  187.8 3.0 conditional.3
  189.3 1.4 convolution_add_fusion
  193.6 3.0 conditional.3
  217.1 5.4 convolution_convert_fusion
  222.6 424.1 %all-reduce.2.cloned.1.call-done = bf16[256,8192]{1,0:T(8,128)(2,1)} async-done(((bf16[256,8192]{1,0:T(8,128)(2,1)}), bf16[256,8192]{1,0:T(8,128)(2,1)}) %all-reduce.2.cloned.1.call-update) | async-done | bytes 4194320 | tf_op jit(solution)/shard_map/psum | solution.py:82
  646.7 1.7 convert_convert_fusion
  (136 shorter events, 44.3 us)
Async XLA Ops:
  6.5 1.0 copy-start
  6.5 71.3 %all-gather.3.cloned.1.call-start = ((), (), s32[]{:S(2)}) async-start(), calls=%async_computation | async-start | bytes 2162688 | tf_op jit(solution)/shard_map/all_gather | solution.py:62
  8.1 135.6 %all-gather.5.cloned.1.call-start = ((), (), s32[]{:S(2)}) async-start(), calls=%async_computation.1 | async-start | bytes 2162688 | tf_op jit(solution)/shard_map/all_gather | solution.py:63
  9.7 637.1 %all-reduce.2.cloned.1.call-start = ((), (), s32[]{:S(2)}) async-start(), calls=%async_computation.2 | async-start | bytes 8388608 | tf_op jit(solution)/shard_map/psum | solution.py:82
Sparse Core Ops, SparseCore 0:
  9.5 68.2 all-gather.2
  79.9 63.8 all-gather.4
  222.7 423.9 all-reduce.1
where the time goes:
time: 656 us; the launch traced here: 655 us
  waiting for transfers between devices  556 us (85%)
  matrix products  46.2 us (7%)
  loops' own time  21.4 us (3%)
  local copies, waits for them, and re-layouts  13.9 us (2%)
  between operations  13.2 us (2%)
    psum x1, waiting for transfers between devices, body(): lax.psum(jnp.dot(attended, out_weight, preferred_element_type=jnp.float32...  424 us
    all_gather x1, waiting for transfers between devices, body(): values_part = lax.all_gather(own_values, 'ctx', axis=0, tiled=True)  66 us
    all_gather x1, waiting for transfers between devices, body(): keys_part = lax.all_gather(local_keys, 'ctx', axis=0, tiled=True)  66 us
    another operation x1, loops' own time, body(): carry, unused = lax.scan(inner, carry, jnp.arange(count // stride))  20.9 us
    dot_general x16, matrix products, update(): allowed = jnp.dot(row_mask, one_hot) > 0.5  15.7 us
  transfers between devices with their start and end apart: 3, of which 3 were waited for; matrix products, arithmetic and copies ran while one was open for 1% of the time, Pallas kernels for 0%

commit v1 on v0

--- a/solution.py
+++ b/solution.py
@@ -59,7 +59,10 @@
         jnp.zeros((heads, rows, HDIM), jnp.float32),
     )
     carry = initial
-    keys_part = lax.all_gather(local_keys, "ctx", axis=0, tiled=True)
+    n_dev = lax.axis_size("ctx")
+    pieces = jnp.stack([local_keys for _ in range(n_dev)])
+    pieces = lax.all_to_all(pieces, "ctx", split_axis=0, concat_axis=0)
+    keys_part = jnp.concatenate(pieces, axis=0)
     values_part = lax.all_gather(own_values, "ctx", axis=0, tiled=True)
     count = keys_part.shape[0]
     stride = 512

time: 656 us -> 602 us (0.918)
  waiting for transfers between devices: 556 us -> 499 us
  starting transfers between devices: 0.09 us -> 9.7 us
  matrix products: 46.2 us -> 37.8 us
    all_gather x1 -> x0, waiting for transfers between devices: 66 us -> none  [body(): keys_part = lax.all_gather(local_keys, 'ctx', axis=0, tiled=True)]
    all_to_all x0 -> x1, starting transfers between devices: none -> 9.62 us  [body(): pieces = lax.all_to_all(pieces, 'ctx', split_axis=0, concat_axis=0)]
    dot_general x9, matrix products: 11.1 us -> 2.91 us  [compute(): jnp.einsum('qhd,kd->hqk', query, keys_part, preferred_element_type=jnp.fl...]
  transfers between devices with their start and end apart: 3 -> 3, of which waited for: 3 -> 2; matrix products, arithmetic and copies ran while one was open for 1% -> 0% of each run, Pallas kernels for 0% -> 0%
where the time goes in v1:
time: 602 us; the launch traced here: 601 us
  waiting for transfers between devices  499 us (83%)
  matrix products  37.8 us (6%)
  loops' own time  22.5 us (4%)
  local copies, waits for them, and re-layouts  14.2 us (2%)
  between operations  13.5 us (2%)
  starting transfers between devices  9.7 us (2%)
    psum x1, waiting for transfers between devices, body(): lax.psum(jnp.dot(attended, out_weight, preferred_element_type=jnp.float32...  428 us
    all_gather x1, waiting for transfers between devices, body(): values_part = lax.all_gather(own_values, 'ctx', axis=0, tiled=True)  71.3 us
    another operation x1, loops' own time, body(): carry, unused = lax.scan(inner, carry, jnp.arange(count // stride))  22 us
    dot_general x16, matrix products, update(): allowed = jnp.dot(row_mask, one_hot) > 0.5  16.3 us
    dot_general x9, matrix products, compute(): jnp.einsum('hqk,kd->hqd', weights.astype(jnp.bfloat16), values_part, pref...  13 us
  transfers between devices with their start and end apart: 3, of which 2 were waited for; matrix products, arithmetic and copies ran while one was open for 0% of the time, Pallas kernels for 0%

profile of v1, /device:TPU:4, one launch (start us, length us, event | category | flops | bytes accessed | tf_op | source)
XLA Modules:
  0.0 601.0 jit_solution(4013968623165272818)
XLA Ops:
  7.5 1.8 stack.2
  9.3 9.6 %all-to-all-start = ((bf16[32,256,128]{2,1,0:T(8,128)(2,1)}), bf16[32,256,128]{2,1,0:T(8,128)(2,1)S(1)}, u32[]{:S(2)}, u32[]{:S(2)}) async-start(bf16[32,256,128]{2,1,0:T(8,128)(2,1)} %stack.2), calls=%async_computation | async-start | bytes 4194304 | tf_op jit(solution)/shard_map/all_to_all | solution.py:64
  19.0 1.5 constant_dynamic-slice_fusion
  21.0 71.3 %all-gather.2.cloned.1.call-done = bf16[8192,128]{1,0:T(8,128)(2,1)} async-done(((bf16[256,128]{1,0:T(8,128)(2,1)}), bf16[8192,128]{1,0:T(8,128)(2,1)}) %all-gather.2.cloned.1.call-update) | async-done | bytes 2097168 | tf_op jit(solution)/shard_map/all_gather | solution.py:66
  92.3 66.7 %while.17 = (s32[]{:T(128)}, f32[2,256]{1,0:T(2,128)S(1)}, f32[2,256]{1,0:T(2,128)S(1)}, f32[2,256,128]{2,1,0:T(8,128)S(1)}, s32[16]{0:T(128)S(1)}, /*index=5*/b...) while((s32[]{:T(128)}, f32[2,256]{1,0:T(2,128)S(1)}, ...), condition=%wide.region_6.7_spmd.clone, body=%wide.region_0.6_spmd.clone.sunk | while | flops 153822208 | bytes 4690489 | solution.py:76
  95.3 2.1 conditional.3
  95.9 1.4 convolution_add_fusion
  100.3 2.1 conditional.3
  100.9 1.4 convolution_add_fusion
  105.4 2.1 conditional.3
  110.5 2.1 conditional.3
  111.1 1.4 convolution_add_fusion
  115.5 2.1 conditional.3
  116.1 1.4 convolution_add_fusion
  120.6 2.1 conditional.3
  121.2 1.4 convolution_add_fusion
  125.7 2.1 conditional.3
  126.3 1.4 convolution_add_fusion
  130.7 2.1 conditional.3
  135.8 2.1 conditional.3
  136.4 1.4 convolution_add_fusion
  159.1 5.4 convolution_convert_fusion
  164.6 427.9 %all-reduce.2.cloned.1.call-done = bf16[256,8192]{1,0:T(8,128)(2,1)} async-done(((bf16[256,8192]{1,0:T(8,128)(2,1)}), bf16[256,8192]{1,0:T(8,128)(2,1)}) %all-reduce.2.cloned.1.call-update) | async-done | bytes 4194320 | tf_op jit(solution)/shard_map/psum | solution.py:85
  592.5 1.7 convert_convert_fusion
  (140 shorter events, 35.8 us)
Async XLA Ops:
  6.5 1.0 copy-start
  6.5 14.0 %copy-start.1 = (bf16[256,256]{1,0:T(8,128)(2,1)S(1)}, bf16[256,256]{1,0:T(8,128)(2,1)}, u32[]{:S(2)}) copy-start(bf16[256,256]{1,0:T(8,128)(2,1)} %param.9) | copy-start | bytes 393220
  6.5 14.2 %copy-start.2 = (s32[64,64]{1,0:T(8,128)S(1)}, s32[64,64]{1,0:T(8,128)}, u32[]{:S(2)}) copy-start(s32[64,64]{1,0:T(8,128)} %param.13) | copy-start | bytes 49156
  9.3 83.0 %all-to-all-start = ((bf16[32,256,128]{2,1,0:T(8,128)(2,1)}), bf16[32,256,128]{2,1,0:T(8,128)(2,1)S(1)}, u32[]{:S(2)}, u32[]{:S(2)}) async-start(bf16[32,256,128]{2,1,0:T(8,128)(2,1)} %stack.2), calls=%async_computation | async-start | bytes 4194304 | tf_op jit(solution)/shard_map/all_to_all | solution.py:64
  18.9 73.3 %all-gather.2.cloned.1.call-start = ((), (), s32[]{:S(2)}) async-start(), calls=%async_computation.1 | async-start | bytes 2162688 | tf_op jit(solution)/shard_map/all_gather | solution.py:66
  20.5 572.0 %all-reduce.2.cloned.1.call-start = ((), (), s32[]{:S(2)}) async-start(), calls=%async_computation.2 | async-start | bytes 8388608 | tf_op jit(solution)/shard_map/psum | solution.py:85
Sparse Core Ops, SparseCore 0:
  21.9 70.3 all-gather.1
  164.7 427.7 all-reduce.1
